TPU v7x, 32 devices: a whole 2x2x4 slice. The times are simulated.
32 devices in a mesh: pix: 16 (over z, y, core), frm: 2 (over x).
Axes of the slice: x: 2, y: 2, z: 4, core: 2. Of those that a mesh axis runs over, the one named last changes fastest.
Arguments:
- frames: bfloat16 [65536, 768], P('pix', 'frm'), may hold values from 0 to 6
- footprints: bfloat16 [65536, 192], P('pix'), may hold values from 0 to 0.024414062
- support: int32 [4096, 192], P('pix'), may hold values 0 or 1
- traces: float32 [1024, 768], P('pix', 'frm'), may hold values from 0 to 2
- block_order: int32 [16, 2], replicated, may hold values from 0 to 1, each once within a row
Outputs:
- refined: bfloat16 [65536, 192], P(('pix', 'frm'))
- updated: float32 [1024, 768], P('pix', 'frm')
Inputs may be any that keep to these rules, and one draw needn't show every extreme that they name: `block_order`: each row lists every block index of a slab once.
All inputs are finite; a program needn't handle non-finite values. No bound on the sum of `support` on one device may be relied on, other than what follows from the above.
Results may differ from a plain program's by a relative error of at most 0.0036.
Values may be sent and summed in bfloat16 or wider, within the bound.
A program may use at most 64 MiB of HBM per device.

v0:
```python
import jax
import jax.numpy as jnp
from jax import lax
from jax.sharding import PartitionSpec as P

BLOCK = 32
TILE = 16


highest = lax.Precision.HIGHEST


def from_behind(block, axis, distance):
    devices = range(lax.axis_size(axis))
    route = [(i - distance, i) for i in devices if i - distance in devices]
    return lax.ppermute(block, axis, route)


def window_mask(support, slab_id, owners, owner_width):
    expanded = jnp.repeat(support, TILE, axis=0).astype(jnp.float32)
    window_of = jnp.arange(3 * owner_width, dtype=jnp.int32) // owner_width
    usable = jnp.where(
        window_of == 0, slab_id > 0, jnp.where(window_of == 2, slab_id < owners - 1, True)
    )
    return expanded * usable.astype(jnp.float32)[None, :]


def trace_block(current, window, drive_rows, coupling, block_id, owner_width):
    row_start = block_id * BLOCK
    band_rows = lax.dynamic_slice_in_dim(coupling, row_start, BLOCK, 0)
    diagonal = jnp.diagonal(
        lax.dynamic_slice_in_dim(band_rows, 2 * owner_width + row_start, BLOCK, 1)
    )
    product = jnp.dot(band_rows, window, precision=highest)
    target = lax.dynamic_slice_in_dim(drive_rows, row_start, BLOCK, 0)
    before = lax.dynamic_slice_in_dim(current, row_start, BLOCK, 0)
    after = jnp.maximum(before + (target - product) / (diagonal[:, None] + 1.0), 0.0)
    return (after, row_start)


def trace_window(current):
    pieces = [from_behind(current, "pix", offset) for offset in (2, 1, -1, -2)]
    return jnp.concatenate([pieces[0], pieces[1], current, pieces[2], pieces[3]], axis=0)


def shards(frames, footprints, support, traces, block_order):
    owners = lax.axis_size("pix")
    slab_id = lax.axis_index("pix")
    owner_width = traces.shape[0]
    sweeps = owner_width // BLOCK
    keep = window_mask(support, slab_id, owners, owner_width)
    active = (footprints.astype(jnp.float32) * keep).astype(jnp.bfloat16)
    loads = jnp.einsum("pk,pt->kt", active, frames, preferred_element_type=jnp.float32)
    correlations = jnp.einsum("pk,pj->kj", active, active, preferred_element_type=jnp.float32)
    drive_rows = loads[owner_width : 2 * owner_width]
    coupling = jnp.pad(
        correlations[owner_width : 2 * owner_width], ((0, 0), (owner_width, owner_width))
    )
    for offset, window_id in ((-1, 0), (1, 2)):
        lower = window_id * owner_width
        arrived = from_behind(
            (loads[lower : lower + owner_width], correlations[lower : lower + owner_width]),
            "pix",
            offset,
        )
        drive_rows = drive_rows + arrived[0]
        if offset == -1:
            coupling = coupling + jnp.pad(arrived[1], ((0, 0), (2 * owner_width, 0)))
        else:
            coupling = coupling + jnp.pad(arrived[1], ((0, 0), (0, 2 * owner_width)))
    current = traces
    for step in range(sweeps):
        window = trace_window(current)
        after, row_start = trace_block(
            current, window, drive_rows, coupling, block_order[slab_id, step], owner_width
        )
        current = lax.dynamic_update_slice_in_dim(current, after, row_start, 0)
    beside = [from_behind(current, "pix", offset) for offset in (1, -1)]
    near_rows = jnp.concatenate([beside[0], current, beside[1]], axis=0)
    rounded = near_rows.astype(jnp.bfloat16)
    shares = lax.axis_size("frm")
    share_rows = footprints.shape[0] // shares
    row_begin = lax.axis_index("frm") * share_rows
    pixel_rows = lax.all_to_all(frames, "frm", split_axis=0, concat_axis=1, tiled=True)
    all_traces = lax.all_gather(rounded, "frm", axis=1, tiled=True)
    mixing = jnp.einsum("pt,kt->pk", pixel_rows, all_traces, preferred_element_type=jnp.float32)
    gram = jnp.einsum("kt,jt->kj", all_traces, all_traces, preferred_element_type=jnp.float32)
    shaped = lax.dynamic_slice_in_dim(active, row_begin, share_rows, 0).astype(jnp.float32)
    keep_rows = lax.dynamic_slice_in_dim(keep, row_begin, share_rows, 0)
    for step in range(sweeps):
        slab_near = jnp.clip(slab_id - 1 + jnp.arange(3, dtype=jnp.int32), 0, owners - 1)
        picked = block_order[slab_near, step]
        columns = (
            jnp.arange(3, dtype=jnp.int32)[:, None] * owner_width
            + picked[:, None] * BLOCK
            + jnp.arange(BLOCK, dtype=jnp.int32)[None, :]
        ).reshape(-1)
        gram_cols = jnp.take(gram, columns, axis=1)
        diagonal = jnp.diagonal(jnp.take(gram_cols, columns, axis=0))
        before = jnp.take(shaped, columns, axis=1)
        target = jnp.take(mixing, columns, axis=1)
        keep_cols = jnp.take(keep_rows, columns, axis=1)
        product = jnp.dot(shaped, gram_cols, precision=highest)
        after = (
            jnp.maximum(before + (target - product) / (diagonal[None, :] + 1.0), 0.0) * keep_cols
        )
        shaped = shaped.at[:, columns].set(after)
    return (shaped.astype(jnp.bfloat16), current)


def solution(mesh):
    in_specs = (P("pix", "frm"), P("pix", None), P("pix", None), P("pix", "frm"), P())
    out_specs = (P(("pix", "frm"), None), P("pix", "frm"))
    return jax.shard_map(shards, mesh=mesh, in_specs=in_specs, out_specs=out_specs, check_vma=False)
```

profile of v0, /device:TPU:10, one launch (start us, length us, event | category | flops | bytes accessed | tf_op | source)
XLA Modules:
  0.0 125.7 jit_solution(3920926233574790244)
XLA Ops:
  0.6 0.9 copy.38
  1.5 2.7 %collective-permute-start.6 = (f32[64,384]{1,0:T(8,128)S(1)}, f32[64,384]{1,0:T(8,128)}, u32[]{:S(2)}, u32[]{:S(2)}) collective-permute-start(f32[64,384]{1,0:T(8,128)S(1)} %copy.38), channel_id=1, source_target_pairs={{2,0},{4,2},{6,4},{8,6},{10,8},{12,10},{14,12},{16,14},{18,16},{20... | collective-permute-start | bytes 294920 | tf_op jit(solution)/shard_map/ppermute | solution.py:16
  4.3 1.9 %collective-permute-start.5 = (f32[64,384]{1,0:T(8,128)S(1)}, f32[64,384]{1,0:T(8,128)}, u32[]{:S(2)}, u32[]{:S(2)}) collective-permute-start(f32[64,384]{1,0:T(8,128)S(1)} %copy.38), channel_id=1, source_target_pairs={{0,2},{2,4},{4,6},{6,8},{8,10},{10,12},{12,14},{14,16},{16,18},{18... | collective-permute-start | bytes 294920 | tf_op jit(solution)/shard_map/ppermute | solution.py:16
  6.2 3.1 %collective-permute-start.4 = (f32[64,384]{1,0:T(8,128)S(1)}, f32[64,384]{1,0:T(8,128)}, u32[]{:S(2)}, u32[]{:S(2)}) collective-permute-start(f32[64,384]{1,0:T(8,128)S(1)} %copy.38), channel_id=1, source_target_pairs={{0,4},{2,6},{4,8},{6,10},{8,12},{10,14},{12,16},{14,18},{16,20},{1... | collective-permute-start | bytes 294920 | tf_op jit(solution)/shard_map/ppermute | solution.py:16
  9.3 5.9 %all-to-all-start = ((bf16[2,2048,384]{2,1,0:T(8,128)(2,1)}), bf16[2,2048,384]{2,1,0:T(8,128)(2,1)}, u32[]{:S(2)}, u32[]{:S(2)}) async-start(bf16[2,2048,384]{2,1,0:T(8,128)(2,1)} %bitcast.56), calls=%async_computation | async-start | bytes 6291456 | tf_op jit(solution)/shard_map/all_to_all | solution.py:84
  15.3 2.3 %broadcast_in_dim.69 = f32[256,16,192]{2,1,0:T(8,128)} broadcast(f32[256,192]{1,0:T(8,128)S(1)} %copy.17), dimensions={0,2} | broadcast | bytes 3342336 | tf_op jit(solution)/shard_map/broadcast_in_dim | solution.py:20
  17.6 5.4 %copy.18 = f32[4096,192]{0,1:T(8,128)} copy(f32[4096,192]{1,0:T(8,128)} %bitcast.55) | data formatting | bytes 6291456 | tf_op jit(solution)/shard_map/convert_element_type | solution.py:20
  23.1 4.4 %multiply_convert_fusion = (bf16[4096,192]{0,1:T(8,128)(2,1)S(1)}, f32[4096,192]{0,1:T(8,128)}) fusion(bf16[4096,192]{0,1:T(8,128)(2,1)S(1)} %copy-done.5, f32[4096,192]{0,1:T(8,128)} %copy.18, f32[192]{0:T(256)S(1)} %select_convert_fusion), kind=kLoop, calls=%fused_computation.18 | loop fusion | flops 3145728 | bytes 9437952 | tf_op jit(solution)/shard_map/convert_element_type | solution.py:52
  28.8 3.3 %collective-permute-start.3 = (f32[64,192]{1,0:T(8,128)}, f32[64,192]{1,0:T(8,128)}, u32[]{:S(2)}, u32[]{:S(2)}) collective-permute-start(f32[64,192]{1,0:T(8,128)} %get-tuple-element.10), channel_id=1, source_target_pairs={{0,2},{2,4},{4,6},{6,8},{8,10},{10,12},{12,14},{14,16},{16,18},{18... | collective-permute-start | bytes 147464 | tf_op jit(solution)/shard_map/ppermute | solution.py:16
  32.1 3.1 %collective-permute-start.2 = (f32[64,192]{1,0:T(8,128)}, f32[64,192]{1,0:T(8,128)}, u32[]{:S(2)}, u32[]{:S(2)}) collective-permute-start(f32[64,192]{1,0:T(8,128)} %get-tuple-element.11), channel_id=1, source_target_pairs={{2,0},{4,2},{6,4},{8,6},{10,8},{12,10},{14,12},{16,14},{18,16},{20... | collective-permute-start | bytes 147464 | tf_op jit(solution)/shard_map/ppermute | solution.py:16
  38.7 2.9 %fusion.32 = f32[192,384]{1,0:T(8,128)S(1)} fusion(bf16[4096,192]{0,1:T(8,128)(2,1)S(1)} %get-tuple-element.4, bf16[4096,384]{1,0:T(8,128)(2,1)} %param.11), kind=kOutput, calls=%fused_computation.100 | convolution fusion | flops 603979776 | bytes 5013504 | tf_op jit(solution)/shard_map/pk,pt->kt/dot_general | solution.py:53
  41.8 1.5 %constant_dynamic-slice_fusion.1 = f32[2048,192]{0,1:T(8,128)S(1)} fusion(f32[4096,192]{0,1:T(8,128)} %get-tuple-element.6, s32[]{:T(128)S(6)} %select_n.126), kind=kLoop, calls=%fused_computation.70 | loop fusion | bytes 3145732 | tf_op jit(solution)/shard_map/dynamic_slice | solution.py:89
  46.5 2.8 %collective-permute-start.7 = (f32[64,384]{1,0:T(8,128)S(1)}, f32[64,384]{1,0:T(8,128)S(1)}, u32[]{:S(2)}, u32[]{:S(2)}) collective-permute-start(f32[64,384]{1,0:T(8,128)S(1)} %copy.38), channel_id=1, source_target_pairs={{4,0},{6,2},{8,4},{10,6},{12,8},{14,10},{16,12},{18,14},{20,16},{2... | collective-permute-start | bytes 294920 | tf_op jit(solution)/shard_map/ppermute | solution.py:16
  49.4 2.7 %collective-permute-start = (f32[64,384]{1,0:T(8,128)}, f32[64,384]{1,0:T(8,128)}, u32[]{:S(2)}, u32[]{:S(2)}) collective-permute-start(f32[64,384]{1,0:T(8,128)} %get-tuple-element.7), channel_id=1, source_target_pairs={{2,0},{4,2},{6,4},{8,6},{10,8},{12,10},{14,12},{16,14},{18,16},{20... | collective-permute-start | bytes 294920 | tf_op jit(solution)/shard_map/ppermute | solution.py:16
  52.1 1.0 pad_add_fusion
  53.2 0.7 gather_fusion.1
  53.9 0.7 gather_fusion.2
  54.7 1.9 %collective-permute-start.1 = (f32[64,384]{1,0:T(8,128)}, f32[64,384]{1,0:T(8,128)S(1)}, u32[]{:S(2)}, u32[]{:S(2)}) collective-permute-start(f32[64,384]{1,0:T(8,128)} %get-tuple-element.8), channel_id=1, source_target_pairs={{0,2},{2,4},{4,6},{6,8},{8,10},{10,12},{12,14},{14,16},{16,18},{18... | collective-permute-start | bytes 294920 | tf_op jit(solution)/shard_map/ppermute | solution.py:16
  56.6 0.9 constant_dynamic-update-slice_fusion.4
  57.5 0.9 constant_dynamic-update-slice_fusion.3
  58.4 0.9 constant_dynamic-update-slice_fusion.1
  59.3 2.4 %collective-permute-done.1 = f32[64,384]{1,0:T(8,128)S(1)} collective-permute-done((f32[64,384]{1,0:T(8,128)}, f32[64,384]{1,0:T(8,128)S(1)}, u32[]{:S(2)}, u32[]{:S(2)}) %collective-permute-start.1) | collective-permute-done | bytes 98336 | tf_op jit(solution)/shard_map/ppermute | solution.py:16
  61.7 1.0 fusion.11
  63.0 1.9 %collective-permute-start.8 = (f32[64,384]{1,0:T(8,128)S(1)}, f32[64,384]{1,0:T(8,128)S(1)}, u32[]{:S(2)}, u32[]{:S(2)}) collective-permute-start(f32[64,384]{1,0:T(8,128)S(1)} %maximum_dynamic-update-slice_fusion.1), channel_id=1, source_target_pairs={{0,4},{2,6},{4,8},{6,10},{8,12},{10,14},{12,16},{14,18},{16,20},{1... | collective-permute-start | bytes 294920 | tf_op jit(solution)/shard_map/ppermute | solution.py:16
  65.0 4.8 %collective-permute-start.11 = (f32[64,384]{1,0:T(8,128)S(1)}, f32[64,384]{1,0:T(8,128)S(1)}, u32[]{:S(2)}, u32[]{:S(2)}) collective-permute-start(f32[64,384]{1,0:T(8,128)S(1)} %maximum_dynamic-update-slice_fusion.1), channel_id=1, source_target_pairs={{4,0},{6,2},{8,4},{10,6},{12,8},{14,10},{16,12},{18,14},{20,16},{2... | collective-permute-start | bytes 294920 | tf_op jit(solution)/shard_map/ppermute | solution.py:16
  69.8 1.9 %collective-permute-start.10 = (f32[64,384]{1,0:T(8,128)S(1)}, f32[64,384]{1,0:T(8,128)S(1)}, u32[]{:S(2)}, u32[]{:S(2)}) collective-permute-start(f32[64,384]{1,0:T(8,128)S(1)} %maximum_dynamic-update-slice_fusion.1), channel_id=1, source_target_pairs={{2,0},{4,2},{6,4},{8,6},{10,8},{12,10},{14,12},{16,14},{18,16},{20... | collective-permute-start | bytes 294920 | tf_op jit(solution)/shard_map/ppermute | solution.py:16
  71.7 2.4 %collective-permute-start.9 = (f32[64,384]{1,0:T(8,128)S(1)}, f32[64,384]{1,0:T(8,128)S(1)}, u32[]{:S(2)}, u32[]{:S(2)}) collective-permute-start(f32[64,384]{1,0:T(8,128)S(1)} %maximum_dynamic-update-slice_fusion.1), channel_id=1, source_target_pairs={{0,2},{2,4},{4,6},{6,8},{8,10},{10,12},{12,14},{14,16},{16,18},{18... | collective-permute-start | bytes 294920 | tf_op jit(solution)/shard_map/ppermute | solution.py:16
  74.2 4.4 %collective-permute-done.9 = f32[64,384]{1,0:T(8,128)S(1)} collective-permute-done((f32[64,384]{1,0:T(8,128)S(1)}, f32[64,384]{1,0:T(8,128)S(1)}, u32[]{:S(2)}, u32[]{:S(2)}) %collective-permute-start.9) | collective-permute-done | bytes 98336 | tf_op jit(solution)/shard_map/ppermute | solution.py:16
  79.1 1.9 %collective-permute-start.13 = (bf16[64,384]{1,0:T(8,128)(2,1)S(1)}, bf16[64,384]{1,0:T(8,128)(2,1)S(1)}, u32[]{:S(2)}, u32[]{:S(2)}) collective-permute-start(bf16[64,384]{1,0:T(8,128)(2,1)S(1)} %convert.27), channel_id=1, source_target_pairs={{2,0},{4,2},{6,4},{8,6},{10,8},{12,10},{14,12},{16,14},{18,16},{20... | collective-permute-start | bytes 147464 | tf_op jit(solution)/shard_map/ppermute | solution.py:16
  81.0 2.4 %collective-permute-start.12 = (bf16[64,384]{1,0:T(8,128)(2,1)S(1)}, bf16[64,384]{1,0:T(8,128)(2,1)S(1)}, u32[]{:S(2)}, u32[]{:S(2)}) collective-permute-start(bf16[64,384]{1,0:T(8,128)(2,1)S(1)} %convert.27), channel_id=1, source_target_pairs={{0,2},{2,4},{4,6},{6,8},{8,10},{10,12},{12,14},{14,16},{16,18},{18... | collective-permute-start | bytes 147464 | tf_op jit(solution)/shard_map/ppermute | solution.py:16
  83.4 1.7 %gather_fusion.15 = f32[96,2048]{1,0:T(8,128)} fusion(f32[2048,192]{0,1:T(8,128)S(1)} %constant_dynamic-slice_fusion.1, s32[1024]{0:T(1024)S(1)} %get-tuple-element.23), kind=kCustom, calls=%fused_computation.7.clone | custom fusion | bytes 1573248 | tf_op jit(solution)/shard_map/jit(_take)/gather | solution.py:102
  85.2 1.7 %gather_fusion.10 = f32[96,2048]{1,0:T(8,128)} fusion(f32[2048,192]{0,1:T(8,128)S(1)} %constant_dynamic-slice_fusion.1, s32[1024]{0:T(1024)S(1)} %get-tuple-element.24), kind=kCustom, calls=%fused_computation.4.clone | custom fusion | bytes 1573248 | tf_op jit(solution)/shard_map/jit(_take)/gather | solution.py:102
  86.9 1.8 %gather_fusion.6 = f32[96,2048]{1,0:T(8,128)} fusion(f32[2048,192]{0,1:T(8,128)S(1)} %dynamic-slice_convert_fusion, s32[1024]{0:T(1024)S(1)} %get-tuple-element.24), kind=kCustom, calls=%fused_computation.clone | custom fusion | bytes 1573248 | tf_op jit(solution)/shard_map/jit(_take)/gather | solution.py:100
  88.7 6.4 %all_gather.3 = bf16[192,768]{1,0:T(8,128)(2,1)S(1)} all-gather(bf16[192,384]{1,0:T(8,128)(2,1)S(1)} %pad_maximum_fusion), channel_id=1, replica_groups=mesh['pix'=16,'frm'=2] {'frm'}, dimensions={1}, use_global_device_ids=true | all-gather | bytes 442368 | tf_op jit(solution)/shard_map/all_gather | solution.py:85
  95.4 0.7 gather_fusion.8
  96.2 0.7 gather_fusion.13
  98.6 1.2 gather_fusion.5
  99.9 1.2 gather_fusion.3
  102.2 4.7 %copy.19 = bf16[2048,2,384]{0,2,1:T(8,128)(2,1)} copy(bf16[2048,2,384]{2,0,1:T(8,128)(2,1)} %bitcast.8) | data formatting | bytes 6291456 | tf_op jit(solution)/shard_map/all_to_all | solution.py:84
  106.9 2.7 %convolution_bitcast_fusion = f32[2048,192]{0,1:T(8,128)S(1)} fusion(bf16[192,768]{1,0:T(8,128)(2,1)S(1)} %all_gather.3, bf16[2048,768]{0,1:T(8,128)(2,1)} %bitcast.57), kind=kOutput, calls=%fused_computation.19 | convolution fusion | flops 603979776 | bytes 5013504 | tf_op jit(solution)/shard_map/pt,kt->pk/dot_general | solution.py:86
  109.6 1.8 %gather_fusion.12 = f32[96,2048]{1,0:T(8,128)} fusion(f32[2048,192]{0,1:T(8,128)S(1)} %convolution_bitcast_fusion, s32[1024]{0:T(1024)S(1)} %get-tuple-element.23), kind=kCustom, calls=%fused_computation.6.clone | custom fusion | bytes 1573248 | tf_op jit(solution)/shard_map/jit(_take)/gather | solution.py:101
  111.5 1.7 %gather_fusion.7 = f32[96,2048]{1,0:T(8,128)} fusion(f32[2048,192]{0,1:T(8,128)S(1)} %convolution_bitcast_fusion, s32[1024]{0:T(1024)S(1)} %get-tuple-element.24), kind=kCustom, calls=%fused_computation.3.clone | custom fusion | bytes 1573248 | tf_op jit(solution)/shard_map/jit(_take)/gather | solution.py:101
  113.2 2.5 %fusion.9 = f32[96,2048]{1,0:T(8,128)S(1)} fusion(f32[96,2048]{1,0:T(8,128)} %gather_fusion.10, f32[96,2048]{1,0:T(8,128)} %gather_fusion.7, f32[96,2048]{1,0:T(8,128)} %gather_fusion.6, bf16[4096,192]{0,1:T(8,128)(2,1)} %copy-done.1, s32[]{:T(128)S(6)} %select_n.126, f32[96]{0:T(128)S(1)} %copy-done.17, pred[96]{0:T(512)(128)(4,1)S(1)} %copy-done.11, ...), kind=kOutput, calls=%fused_computation.31 | convolution fusion | flops 454576128 | bytes 4032004 | tf_op jit(solution)/shard_map/dot_general | solution.py:103
  115.8 1.7 %scatter_fusion = f32[2048,192]{0,1:T(8,128)S(1)} fusion(f32[2048,192]{0,1:T(8,128)S(1)} %dynamic-slice_convert_fusion, s32[96]{0:T(128)S(1)} %copy-done.13, f32[96,2048]{1,0:T(8,128)S(1)} %fusion.9), kind=kCustom, calls=%fused_computation.16 | custom fusion | bytes 2359680 | tf_op jit(solution)/shard_map/scatter | solution.py:107
  117.4 1.7 %gather_fusion.11 = f32[96,2048]{1,0:T(8,128)} fusion(f32[2048,192]{0,1:T(8,128)S(1)} %scatter_fusion, s32[1024]{0:T(1024)S(1)} %get-tuple-element.23), kind=kCustom, calls=%fused_computation.5.clone | custom fusion | bytes 1573248 | tf_op jit(solution)/shard_map/jit(_take)/gather | solution.py:100
  119.2 3.2 %fusion.5 = f32[96,2048]{1,0:T(8,128)} fusion(f32[2048,192]{0,1:T(8,128)S(1)} %scatter_fusion, f32[96,2048]{1,0:T(8,128)S(1)} %copy-done.2, f32[96,2048]{1,0:T(8,128)S(1)} %copy-done.3, f32[96,2048]{1,0:T(8,128)} %gather_fusion.11, f32[96]{0:T(128)S(1)} %copy-done.16, pred[96]{0:T(512)(128)(4,1)S(1)} %get-tuple-element.19, f32[96,192]{1,0:T(8,128)S(1)} %gather_fusion.13), kind=kOutput, calls=%fused_computation.27 | convolution fusion | flops 454576128 | bytes 4792800 | tf_op jit(solution)/shard_map/dot_general | solution.py:103
  122.4 2.2 %scatter_fusion.1 = f32[2048,192]{0,1:T(8,128)S(1)} fusion(f32[2048,192]{0,1:T(8,128)S(1)} %scatter_fusion, s32[96]{0:T(128)S(1)} %copy-done.12, f32[96,2048]{1,0:T(8,128)} %fusion.5), kind=kCustom, calls=%fused_computation.17 | custom fusion | bytes 2359680 | tf_op jit(solution)/shard_map/scatter | solution.py:107
  124.7 1.0 convert_element_type.39
  (101 shorter events, 11.1 us)
Async XLA Ops:
  1.5 56.9 %collective-permute-start.6 = (f32[64,384]{1,0:T(8,128)S(1)}, f32[64,384]{1,0:T(8,128)}, u32[]{:S(2)}, u32[]{:S(2)}) collective-permute-start(f32[64,384]{1,0:T(8,128)S(1)} %copy.38), channel_id=1, source_target_pairs={{2,0},{4,2},{6,4},{8,6},{10,8},{12,10},{14,12},{16,14},{18,16},{20... | collective-permute-start | bytes 294920 | tf_op jit(solution)/shard_map/ppermute | solution.py:16
  4.3 53.2 %collective-permute-start.5 = (f32[64,384]{1,0:T(8,128)S(1)}, f32[64,384]{1,0:T(8,128)}, u32[]{:S(2)}, u32[]{:S(2)}) collective-permute-start(f32[64,384]{1,0:T(8,128)S(1)} %copy.38), channel_id=1, source_target_pairs={{0,2},{2,4},{4,6},{6,8},{8,10},{10,12},{12,14},{14,16},{16,18},{18... | collective-permute-start | bytes 294920 | tf_op jit(solution)/shard_map/ppermute | solution.py:16
  6.2 48.5 %collective-permute-start.4 = (f32[64,384]{1,0:T(8,128)S(1)}, f32[64,384]{1,0:T(8,128)}, u32[]{:S(2)}, u32[]{:S(2)}) collective-permute-start(f32[64,384]{1,0:T(8,128)S(1)} %copy.38), channel_id=1, source_target_pairs={{0,4},{2,6},{4,8},{6,10},{8,12},{10,14},{12,16},{14,18},{16,20},{1... | collective-permute-start | bytes 294920 | tf_op jit(solution)/shard_map/ppermute | solution.py:16
  9.3 5.9 %copy-start.9 = (s32[256,192]{0,1:T(8,128)S(1)}, s32[256,192]{0,1:T(8,128)}, u32[]{:S(2)}) copy-start(s32[256,192]{0,1:T(8,128)} %param.13) | copy-start | bytes 589828
  9.3 92.9 %all-to-all-start = ((bf16[2,2048,384]{2,1,0:T(8,128)(2,1)}), bf16[2,2048,384]{2,1,0:T(8,128)(2,1)}, u32[]{:S(2)}, u32[]{:S(2)}) async-start(bf16[2,2048,384]{2,1,0:T(8,128)(2,1)} %bitcast.56), calls=%async_computation | async-start | bytes 6291456 | tf_op jit(solution)/shard_map/all_to_all | solution.py:84
  17.6 5.5 %copy-start.5 = (bf16[4096,192]{0,1:T(8,128)(2,1)S(1)}, bf16[4096,192]{0,1:T(8,128)(2,1)}, u32[]{:S(2)}) copy-start(bf16[4096,192]{0,1:T(8,128)(2,1)} %param.12) | copy-start | bytes 4718596
  27.5 14.1 %copy-start.1 = (bf16[4096,192]{0,1:T(8,128)(2,1)}, bf16[4096,192]{0,1:T(8,128)(2,1)S(1)}, u32[]{:S(2)}) copy-start(bf16[4096,192]{0,1:T(8,128)(2,1)S(1)} %get-tuple-element.4) | copy-start | bytes 4718596
  27.5 7.8 %copy-start = (s32[16,2]{0,1:T(2,128)S(1)}, s32[16,2]{0,1:T(2,128)}, u32[]{:S(2)}) copy-start(s32[16,2]{0,1:T(2,128)} %param.15) | copy-start | bytes 388
  28.8 17.8 %collective-permute-start.3 = (f32[64,192]{1,0:T(8,128)}, f32[64,192]{1,0:T(8,128)}, u32[]{:S(2)}, u32[]{:S(2)}) collective-permute-start(f32[64,192]{1,0:T(8,128)} %get-tuple-element.10), channel_id=1, source_target_pairs={{0,2},{2,4},{4,6},{6,8},{8,10},{10,12},{12,14},{14,16},{16,18},{18... | collective-permute-start | bytes 147464 | tf_op jit(solution)/shard_map/ppermute | solution.py:16
  32.1 17.3 %collective-permute-start.2 = (f32[64,192]{1,0:T(8,128)}, f32[64,192]{1,0:T(8,128)}, u32[]{:S(2)}, u32[]{:S(2)}) collective-permute-start(f32[64,192]{1,0:T(8,128)} %get-tuple-element.11), channel_id=1, source_target_pairs={{2,0},{4,2},{6,4},{8,6},{10,8},{12,10},{14,12},{16,14},{18,16},{20... | collective-permute-start | bytes 147464 | tf_op jit(solution)/shard_map/ppermute | solution.py:16
  41.6 1.7 %copy-start.6 = (f32[192,384]{1,0:T(8,128)}, f32[192,384]{1,0:T(8,128)S(1)}, u32[]{:S(2)}) copy-start(f32[192,384]{1,0:T(8,128)S(1)} %fusion.32) | copy-start | bytes 884740
  41.8 2.8 %copy-start.14 = (s32[96]{0:T(128)S(1)}, s32[96]{0:T(128)}, u32[]{:S(2)}) copy-start(s32[96]{0:T(128)} %compare_select_fusion) | copy-start | bytes 1156
  41.8 2.8 %copy-start.15 = (s32[96]{0:T(128)S(1)}, s32[96]{0:T(128)}, u32[]{:S(2)}) copy-start(s32[96]{0:T(128)} %compare_select_fusion.1) | copy-start | bytes 1156
  46.5 12.8 %collective-permute-start.7 = (f32[64,384]{1,0:T(8,128)S(1)}, f32[64,384]{1,0:T(8,128)S(1)}, u32[]{:S(2)}, u32[]{:S(2)}) collective-permute-start(f32[64,384]{1,0:T(8,128)S(1)} %copy.38), channel_id=1, source_target_pairs={{4,0},{6,2},{8,4},{10,6},{12,8},{14,10},{16,12},{18,14},{20,16},{2... | collective-permute-start | bytes 294920 | tf_op jit(solution)/shard_map/ppermute | solution.py:16
  49.4 10.0 %collective-permute-start = (f32[64,384]{1,0:T(8,128)}, f32[64,384]{1,0:T(8,128)}, u32[]{:S(2)}, u32[]{:S(2)}) collective-permute-start(f32[64,384]{1,0:T(8,128)} %get-tuple-element.7), channel_id=1, source_target_pairs={{2,0},{4,2},{6,4},{8,6},{10,8},{12,10},{14,12},{16,14},{18,16},{20... | collective-permute-start | bytes 294920 | tf_op jit(solution)/shard_map/ppermute | solution.py:16
  54.7 7.0 %collective-permute-start.1 = (f32[64,384]{1,0:T(8,128)}, f32[64,384]{1,0:T(8,128)S(1)}, u32[]{:S(2)}, u32[]{:S(2)}) collective-permute-start(f32[64,384]{1,0:T(8,128)} %get-tuple-element.8), channel_id=1, source_target_pairs={{0,2},{2,4},{4,6},{6,8},{8,10},{10,12},{12,14},{14,16},{16,18},{18... | collective-permute-start | bytes 294920 | tf_op jit(solution)/shard_map/ppermute | solution.py:16
  63.0 11.1 %collective-permute-start.8 = (f32[64,384]{1,0:T(8,128)S(1)}, f32[64,384]{1,0:T(8,128)S(1)}, u32[]{:S(2)}, u32[]{:S(2)}) collective-permute-start(f32[64,384]{1,0:T(8,128)S(1)} %maximum_dynamic-update-slice_fusion.1), channel_id=1, source_target_pairs={{0,4},{2,6},{4,8},{6,10},{8,12},{10,14},{12,16},{14,18},{16,20},{1... | collective-permute-start | bytes 294920 | tf_op jit(solution)/shard_map/ppermute | solution.py:16
  65.0 13.7 %collective-permute-start.11 = (f32[64,384]{1,0:T(8,128)S(1)}, f32[64,384]{1,0:T(8,128)S(1)}, u32[]{:S(2)}, u32[]{:S(2)}) collective-permute-start(f32[64,384]{1,0:T(8,128)S(1)} %maximum_dynamic-update-slice_fusion.1), channel_id=1, source_target_pairs={{4,0},{6,2},{8,4},{10,6},{12,8},{14,10},{16,12},{18,14},{20,16},{2... | collective-permute-start | bytes 294920 | tf_op jit(solution)/shard_map/ppermute | solution.py:16
  69.8 8.8 %collective-permute-start.10 = (f32[64,384]{1,0:T(8,128)S(1)}, f32[64,384]{1,0:T(8,128)S(1)}, u32[]{:S(2)}, u32[]{:S(2)}) collective-permute-start(f32[64,384]{1,0:T(8,128)S(1)} %maximum_dynamic-update-slice_fusion.1), channel_id=1, source_target_pairs={{2,0},{4,2},{6,4},{8,6},{10,8},{12,10},{14,12},{16,14},{18,16},{20... | collective-permute-start | bytes 294920 | tf_op jit(solution)/shard_map/ppermute | solution.py:16
  71.7 6.8 %collective-permute-start.9 = (f32[64,384]{1,0:T(8,128)S(1)}, f32[64,384]{1,0:T(8,128)S(1)}, u32[]{:S(2)}, u32[]{:S(2)}) collective-permute-start(f32[64,384]{1,0:T(8,128)S(1)} %maximum_dynamic-update-slice_fusion.1), channel_id=1, source_target_pairs={{0,2},{2,4},{4,6},{6,8},{8,10},{10,12},{12,14},{14,16},{16,18},{18... | collective-permute-start | bytes 294920 | tf_op jit(solution)/shard_map/ppermute | solution.py:16
  79.1 6.1 %copy-start.4 = (f32[64,384]{1,0:T(8,128)}, f32[64,384]{1,0:T(8,128)S(1)}, u32[]{:S(2)}) copy-start(f32[64,384]{1,0:T(8,128)S(1)} %maximum_dynamic-update-slice_fusion) | copy-start | bytes 294916
  79.1 9.6 %collective-permute-start.13 = (bf16[64,384]{1,0:T(8,128)(2,1)S(1)}, bf16[64,384]{1,0:T(8,128)(2,1)S(1)}, u32[]{:S(2)}, u32[]{:S(2)}) collective-permute-start(bf16[64,384]{1,0:T(8,128)(2,1)S(1)} %convert.27), channel_id=1, source_target_pairs={{2,0},{4,2},{6,4},{8,6},{10,8},{12,10},{14,12},{16,14},{18,16},{20... | collective-permute-start | bytes 147464 | tf_op jit(solution)/shard_map/ppermute | solution.py:16
  81.0 7.7 %collective-permute-start.12 = (bf16[64,384]{1,0:T(8,128)(2,1)S(1)}, bf16[64,384]{1,0:T(8,128)(2,1)S(1)}, u32[]{:S(2)}, u32[]{:S(2)}) collective-permute-start(bf16[64,384]{1,0:T(8,128)(2,1)S(1)} %convert.27), channel_id=1, source_target_pairs={{0,2},{2,4},{4,6},{6,8},{8,10},{10,12},{12,14},{14,16},{16,18},{18... | collective-permute-start | bytes 147464 | tf_op jit(solution)/shard_map/ppermute | solution.py:16
  95.2 2.5 %copy-start.10 = (pred[96]{0:T(512)(128)(4,1)S(1)}, pred[96]{0:T(512)(128)(4,1)}, u32[]{:S(2)}) copy-start(pred[96]{0:T(512)(128)(4,1)} %get-tuple-element.20) | copy-start | bytes 292
  96.1 3.7 %copy-start.7 = (f32[96,192]{1,0:T(8,128)}, f32[96,192]{1,0:T(8,128)S(1)}, u32[]{:S(2)}) copy-start(f32[96,192]{1,0:T(8,128)S(1)} %gather_fusion.8) | copy-start | bytes 221188
  111.4 1.7 %copy-start.8 = (f32[96,192]{1,0:T(8,128)S(1)}, f32[96,192]{1,0:T(8,128)}, u32[]{:S(2)}) copy-start(f32[96,192]{1,0:T(8,128)} %copy-done.7) | copy-start | bytes 221188
  111.4 1.7 %copy-start.11 = (pred[96]{0:T(512)(128)(4,1)S(1)}, pred[96]{0:T(512)(128)(4,1)}, u32[]{:S(2)}) copy-start(pred[96]{0:T(512)(128)(4,1)} %get-tuple-element.20) | copy-start | bytes 292
  111.5 1.7 %copy-start.17 = (f32[96]{0:T(128)S(1)}, f32[96]{0:T(128)}, u32[]{:S(2)}) copy-start(f32[96]{0:T(128)} %broadcast_add_fusion.1) | copy-start | bytes 1156
  113.2 2.6 %copy-start.13 = (s32[96]{0:T(128)S(1)}, s32[96]{0:T(128)}, u32[]{:S(2)}) copy-start(s32[96]{0:T(128)} %get-tuple-element.21) | copy-start | bytes 1156
  117.4 1.8 %copy-start.2 = (f32[96,2048]{1,0:T(8,128)S(1)}, f32[96,2048]{1,0:T(8,128)}, u32[]{:S(2)}) copy-start(f32[96,2048]{1,0:T(8,128)} %gather_fusion.15) | copy-start | bytes 2359300
  117.4 1.8 %copy-start.3 = (f32[96,2048]{1,0:T(8,128)S(1)}, f32[96,2048]{1,0:T(8,128)}, u32[]{:S(2)}) copy-start(f32[96,2048]{1,0:T(8,128)} %gather_fusion.12) | copy-start | bytes 2359300
  117.4 1.7 %copy-start.16 = (f32[96]{0:T(128)S(1)}, f32[96]{0:T(128)}, u32[]{:S(2)}) copy-start(f32[96]{0:T(128)} %broadcast_add_fusion) | copy-start | bytes 1156
  119.2 3.2 %copy-start.12 = (s32[96]{0:T(128)S(1)}, s32[96]{0:T(128)}, u32[]{:S(2)}) copy-start(s32[96]{0:T(128)} %get-tuple-element.22) | copy-start | bytes 1156
where the time goes:
time: 127 us; the launch traced here: 126 us
  starting transfers between devices  42.9 us (34%)
  local copies, waits for them, and re-layouts  42.8 us (34%)
  matrix products  12.9 us (10%)
  other arithmetic  11.3 us (9%)
  waiting for transfers between devices  6.78 us (5%)
  blocking collectives  6.44 us (5%)
  between operations  2.49 us (2%)
    ppermute x14, starting transfers between devices, from_behind(): return lax.ppermute(block, axis, route)  37.1 us
    ppermute x14, waiting for transfers between devices, from_behind(): return lax.ppermute(block, axis, route)  6.78 us
    all_gather x1, blocking collectives, shards(): all_traces = lax.all_gather(rounded, 'frm', axis=1, tiled=True)  6.44 us
    all_to_all x1, starting transfers between devices, shards(): lax.all_to_all(frames, 'frm', split_axis=0, concat_axis=1, tiled=True)  5.87 us
    dot_general x2, matrix products, shards(): product = jnp.dot(shaped, gram_cols, precision=highest)  5.75 us
    convert_element_type x2, local copies, waits for them, and re-layouts, window_mask(): expanded = jnp.repeat(support, TILE, axis=0).astype(jnp.float32)  5.58 us
    all_to_all x1, local copies, waits for them, and re-layouts, shards(): lax.all_to_all(frames, 'frm', split_axis=0, concat_axis=1, tiled=True)  4.7 us
    convert_element_type x1, other arithmetic, shards(): active = (footprints.astype(jnp.float32) * keep).astype(jnp.bfloat16)  4.39 us
  transfers between devices with their start and end apart: 15, of which 2 were waited for; matrix products, arithmetic and copies ran while one was open for 34% of the time, Pallas kernels for 0%

commit v1 on v0

v1 whole, which is shorter than its diff:
```python
import functools

import jax
import jax.numpy as jnp
from jax import lax
from jax.experimental import pallas as pl
from jax.experimental.pallas import tpu as pltpu
from jax.sharding import PartitionSpec as P

BLOCK = 32
TILE = 16
MESH = pl.DeviceIdType.MESH
OFFSETS = (-2, -1, 1, 2)
f32, bf16 = jnp.float32, jnp.bfloat16


def dot(a, b, dims=((1,), (0,))):
    return lax.dot_general(a, b, (dims, ((), ())), preferred_element_type=f32)


def halves(x):
    high = x.astype(bf16)
    return high, (x - high.astype(f32)).astype(bf16)


def kernel(
    owners, shares, order_ref, frames_ref, foot_ref, support_ref, traces_ref, refined_ref, updated_ref,
    act, keep, pc, side, win, blk_out, blk_in, near, gram_own, gram_in, part_own, part_out, part_in,
    a_send, a_recv, b_send, b_recv, c_send, c_recv, d_send, d_recv, g_send, g_recv, f_send, f_recv,
):
    slab, mine = lax.axis_index("pix"), lax.axis_index("frm")
    pixels, frames_here = frames_ref.shape
    width = traces_ref.shape[0]
    three = 3 * width
    sweeps = width // BLOCK
    share_rows = pixels // shares
    barrier = pltpu.get_barrier_semaphore()

    def present(offset):
        return slab + offset >= 0 if offset < 0 else slab + offset < owners

    def slot(offset):
        return OFFSETS.index(offset)

    def partner(d):
        return lax.rem(mine + d, shares)

    for offset in OFFSETS:
        @pl.when(present(offset))
        def _():
            pl.semaphore_signal(barrier, inc=1, device_id=(slab + offset, mine), device_id_type=MESH)

        @pl.when(jnp.logical_not(present(offset)))
        def _():
            row = (2 + offset) * width
            win[row : row + width, :] = jnp.zeros((width, frames_here), f32)
            for step in range(sweeps - 1):
                blk_in[step, slot(offset)] = jnp.zeros((BLOCK, frames_here), f32)
            if abs(offset) == 1:
                at = 0 if offset < 0 else 1
                side[at] = jnp.zeros(side.shape[1:], f32)
                row = (1 + offset) * width
                near[row : row + width, :] = jnp.zeros((width, frames_here), bf16)
    for d in range(1, shares):
        pl.semaphore_signal(barrier, inc=1, device_id=(slab, partner(d)), device_id_type=MESH)

    win[2 * width : 3 * width, :] = traces_ref[...]

    peers = jnp.minimum(slab, 2) + jnp.minimum(owners - 1 - slab, 2) + shares - 1
    pl.semaphore_wait(barrier, peers)

    def send_traces(offset):
        row = (2 - offset) * width
        k = slot(-offset)
        return pltpu.make_async_remote_copy(
            src_ref=traces_ref, dst_ref=win.at[pl.ds(row, width)], send_sem=a_send.at[k],
            recv_sem=a_recv.at[k], device_id=(slab + offset, mine), device_id_type=MESH)

    def send_side(offset):
        at = 1 if offset < 0 else 0
        row = 0 if offset < 0 else 2 * width
        return pltpu.make_async_remote_copy(
            src_ref=pc.at[pl.ds(row, width)], dst_ref=side.at[at], send_sem=b_send.at[at],
            recv_sem=b_recv.at[at], device_id=(slab + offset, mine), device_id_type=MESH)

    def send_block(step, offset):
        k = slot(-offset)
        return pltpu.make_async_remote_copy(
            src_ref=blk_out.at[step], dst_ref=blk_in.at[step, k], send_sem=c_send.at[step, k],
            recv_sem=c_recv.at[step, k], device_id=(slab + offset, mine), device_id_type=MESH)

    def send_near(offset):
        at = 1 if offset < 0 else 0
        row = (1 - offset) * width
        return pltpu.make_async_remote_copy(
            src_ref=near.at[pl.ds(width, width)], dst_ref=near.at[pl.ds(row, width)], send_sem=d_send.at[at],
            recv_sem=d_recv.at[at], device_id=(slab + offset, mine), device_id_type=MESH)

    def send_gram(d):
        return pltpu.make_async_remote_copy(
            src_ref=gram_own, dst_ref=gram_in.at[d - 1], send_sem=g_send.at[d - 1],
            recv_sem=g_recv.at[d - 1], device_id=(slab, partner(d)), device_id_type=MESH)

    pieces, rows_each = part_out.shape[1], part_out.shape[3]

    def send_part(d, piece):
        return pltpu.make_async_remote_copy(
            src_ref=part_out.at[d - 1, piece], dst_ref=part_in.at[d - 1, piece], send_sem=f_send.at[d - 1, piece],
            recv_sem=f_recv.at[d - 1, piece], device_id=(slab, partner(d)), device_id_type=MESH)

    def start(copy, offset):
        @pl.when(present(offset))
        def _():
            copy(offset).start()

    def arrive(copy, offset):
        @pl.when(present(-offset))
        def _():
            copy(offset).wait_recv()

    def left(copy, offset):
        @pl.when(present(offset))
        def _():
            copy(offset).wait_send()

    for offset in OFFSETS:
        start(send_traces, offset)

    line = lax.broadcasted_iota(jnp.int32, (three, 1), 0)
    window_of = line // width
    usable = jnp.where(
        window_of == 0, (slab > 0).astype(f32), jnp.where(window_of == 2, (slab < owners - 1).astype(f32), 1.0))
    supported = (support_ref[...].astype(f32) * usable).astype(bf16)

    chunk = min(pixels, 512)
    tiles = support_ref.shape[1]
    pc[...] = jnp.zeros(pc.shape, f32)
    tile_of = lax.broadcasted_iota(jnp.int32, (tiles, chunk), 1) // TILE
    tile_is = lax.broadcasted_iota(jnp.int32, (tiles, chunk), 0)

    def project(c, carry):
        rows = pl.ds(pl.multiple_of(c * chunk, chunk), chunk)
        spread = (tile_is == tile_of + c * (chunk // TILE)).astype(f32).astype(bf16)
        mask = dot(supported, spread).astype(bf16)
        active = foot_ref[:, rows] * mask
        keep[:, rows] = mask
        act[:, rows] = active
        pc[:, :frames_here] += dot(active, frames_ref[rows, :])
        pc[:, frames_here : frames_here + three] += dot(active, active, ((1,), (1,)))
        return carry

    lax.fori_loop(0, pixels // chunk, project, 0)
    for offset in (-1, 1):
        start(send_side, offset)
    for offset in OFFSETS:
        arrive(send_traces, offset)
    for offset in (-1, 1):
        arrive(send_side, offset)

    own = pc[width : 2 * width, :]
    loads = own[:, :frames_here] + side[0][:, :frames_here] + side[1][:, :frames_here]
    parts = [side[0][:, frames_here : frames_here + three], own[:, frames_here : frames_here + three],
             side[1][:, frames_here : frames_here + three]]
    row = lax.broadcasted_iota(jnp.int32, (width, three), 0)
    column = lax.broadcasted_iota(jnp.int32, (width, three), 1)
    diagonal = jnp.zeros((width, 1), f32)
    stacked, tops = [], []
    for i, part in enumerate(parts):
        diagonal += jnp.sum(jnp.where(column == row + (2 - i) * width, part, 0.0), axis=1, keepdims=True)
        high, low = halves(part)
        tops.append(high)
        stacked.append(jnp.concatenate([high, low], axis=0))
    block_of = lax.broadcasted_iota(jnp.int32, (width, 1), 0) // BLOCK

    for step in range(sweeps):
        if step > 0:
            for offset in OFFSETS:
                arrive(functools.partial(send_block, step - 1), offset)
            for offset in OFFSETS:
                there = jnp.clip(slab + offset, 0, owners - 1)
                first = (2 + offset) * width
                news = jnp.concatenate([blk_in[step - 1, slot(offset)]] * sweeps, axis=0)
                win[first : first + width, :] = jnp.where(
                    block_of == order_ref[step - 1, there], news, win[first : first + width, :])
        high, low = halves(win[...])
        product = jnp.zeros((width, frames_here), f32)
        for i in range(3):
            span = slice(i * width, i * width + three)
            both = dot(stacked[i], high[span])
            product += both[:width] + both[width:] + dot(tops[i], low[span])
        before = win[2 * width : 3 * width, :]
        after = jnp.maximum(before + (loads - product) / (diagonal + 1.0), 0.0)
        picked = order_ref[step, slab]
        if step < sweeps - 1:
            block = jnp.zeros((BLOCK, frames_here), f32)
            for k in range(sweeps):
                block = jnp.where(picked == k, after[k * BLOCK : (k + 1) * BLOCK], block)
            blk_out[step] = block
            for offset in OFFSETS:
                start(functools.partial(send_block, step), offset)
        current = jnp.where(block_of == picked, after, before)
        if step < sweeps - 1:
            win[2 * width : 3 * width, :] = current
        else:
            near[width : 2 * width, :] = current.astype(bf16)
            for offset in (-1, 1):
                start(send_near, offset)
            updated_ref[...] = current

    for offset in (-1, 1):
        arrive(send_near, offset)
    traces_near = near[...]
    gram_here = dot(traces_near, traces_near, ((1,), (1,)))
    gram_own[...] = gram_here
    for d in range(1, shares):
        send_gram(d).start()
    both = jnp.concatenate(halves(gram_here), axis=0)

    def residual(first):
        rows = pl.ds(pl.multiple_of(first, rows_each), rows_each)
        fitted = dot(both, act[:, rows])
        return dot(traces_near, frames_ref[rows, :], ((1,), (1,))) - fitted[:three] - fitted[three:]

    for piece in range(pieces):
        for d in range(1, shares):
            part_out[d - 1, piece] = residual(partner(d) * share_rows + piece * rows_each).astype(bf16)
            send_part(d, piece).start()
    for piece in range(pieces):
        part_own[piece] = residual(mine * share_rows + piece * rows_each)

    gram = gram_here
    for d in range(1, shares):
        send_gram(d).wait_recv()
        gram += gram_in[d - 1]
    grow = lax.broadcasted_iota(jnp.int32, (three, three), 0)
    gcol = lax.broadcasted_iota(jnp.int32, (three, three), 1)
    rate = 1.0 / (jnp.sum(jnp.where(grow == gcol, gram, 0.0), axis=1, keepdims=True) + 1.0)
    gram_high, gram_low = halves(gram)
    gram_both = jnp.concatenate([gram_high, gram_low], axis=0)
    line_block = lax.rem(line, width) // BLOCK
    picks = []
    for step in range(sweeps):
        chosen = [order_ref[step, jnp.clip(slab - 1 + w, 0, owners - 1)] for w in range(3)]
        chosen = jnp.where(window_of == 0, chosen[0], jnp.where(window_of == 1, chosen[1], chosen[2]))
        picks.append(line_block == chosen)

    for piece in range(pieces):
        left_over = part_own[piece]
        for d in range(1, shares):
            send_part(d, piece).wait_recv()
            left_over += part_in[d - 1, piece].astype(f32)
        here = pl.ds(pl.multiple_of(mine * share_rows + piece * rows_each, rows_each), rows_each)
        shaped = act[:, here].astype(f32)
        mask = keep[:, here].astype(f32)
        for step in range(sweeps):
            after = jnp.where(picks[step], jnp.maximum(shaped + left_over * rate, 0.0) * mask, shaped)
            if step < sweeps - 1:
                moved, rest = halves(after - shaped)
                change = dot(gram_both, moved)
                left_over -= change[:three] + change[three:] + dot(gram_high, rest)
            shaped = after
        refined_ref[:, piece * rows_each : (piece + 1) * rows_each] = shaped.astype(bf16)

    for offset in OFFSETS:
        left(send_traces, offset)
        for step in range(sweeps - 1):
            left(functools.partial(send_block, step), offset)
    for offset in (-1, 1):
        left(send_side, offset)
        left(send_near, offset)
    for d in range(1, shares):
        send_gram(d).wait_send()
        for piece in range(pieces):
            send_part(d, piece).wait_send()


def shards(owners, shares, frames, footprints, support, traces, block_order):
    pixels, frames_here = frames.shape
    width = traces.shape[0]
    three = 3 * width
    rounds = max(width // BLOCK - 1, 1)
    share_rows = pixels // shares
    rows_each = min(share_rows, 512)
    pieces = share_rows // rows_each
    others = max(shares - 1, 1)
    side_width = -(-(frames_here + three) // 128) * 128
    vmem, dma = pltpu.VMEM, pltpu.SemaphoreType.DMA
    refined, updated = pl.pallas_call(
        functools.partial(kernel, owners, shares),
        out_shape=(
            jax.ShapeDtypeStruct((three, share_rows), bf16),
            jax.ShapeDtypeStruct(traces.shape, f32),
        ),
        in_specs=[pl.BlockSpec(memory_space=pltpu.SMEM)] + [pl.BlockSpec(memory_space=vmem)] * 4,
        out_specs=(pl.BlockSpec(memory_space=vmem), pl.BlockSpec(memory_space=vmem)),
        scratch_shapes=[
            vmem((three, pixels), bf16),
            vmem((three, pixels), bf16),
            vmem((three, side_width), f32),
            vmem((2, width, side_width), f32),
            vmem((5 * width, frames_here), f32),
            vmem((rounds, BLOCK, frames_here), f32),
            vmem((rounds, 4, BLOCK, frames_here), f32),
            vmem((three, frames_here), bf16),
            vmem((three, three), f32),
            vmem((others, three, three), f32),
            vmem((pieces, three, rows_each), f32),
            vmem((others, pieces, three, rows_each), bf16),
            vmem((others, pieces, three, rows_each), bf16),
            dma((4,)), dma((4,)), dma((2,)), dma((2,)),
            dma((rounds, 4)), dma((rounds, 4)), dma((2,)), dma((2,)),
            dma((others,)), dma((others,)), dma((others, pieces)), dma((others, pieces)),
        ],
        compiler_params=pltpu.CompilerParams(
            collective_id=0, has_side_effects=True, vmem_limit_bytes=48 * 1024 * 1024
        ),
    )(block_order.T, frames, footprints.T, support.T, traces)
    return refined.T, updated


def solution(mesh):
    in_specs = (P("pix", "frm"), P("pix", None), P("pix", None), P("pix", "frm"), P())
    out_specs = (P(("pix", "frm"), None), P("pix", "frm"))
    body = functools.partial(shards, mesh.shape["pix"], mesh.shape["frm"])
    return jax.shard_map(body, mesh=mesh, in_specs=in_specs, out_specs=out_specs, check_vma=False)
```

time: 127 us -> 54.5 us (0.43)
  the two profiles are of different devices: /device:TPU:10 before, /device:TPU:16 now
where the time goes in v1:
time: 54.5 us; the launch traced here: 54.3 us
  Pallas kernels  46.3 us (85%)
  local copies, waits for them, and re-layouts  7.31 us (13%)
  between operations  0.65 us (1%)
    pallas_call x1, Pallas kernels, shards(): pl.pallas_call(functools.partial(kernel, owners, shares), out_shape=(jax....  46.3 us
    unnamed x12, local copies, waits for them, and re-layouts  7.31 us

profile of v1, /device:TPU:16, one launch (start us, length us, event | category | flops | bytes accessed | tf_op | source)
XLA Modules:
  0.0 54.3 jit_solution(5859022722212810474)
XLA Ops:
  0.6 0.0 copy-start
  0.6 1.9 %copy-done = bf16[4096,384]{1,0:T(8,128)(2,1)S(1)} copy-done((bf16[4096,384]{1,0:T(8,128)(2,1)S(1)}, bf16[4096,384]{1,0:T(8,128)(2,1)}, u32[]{:S(2)}) %copy-start) | copy-done | bytes 3145752
  2.5 0.0 copy-start.1
  2.5 1.4 %copy-done.1 = bf16[4096,192]{0,1:T(8,128)(2,1)S(1)} copy-done((bf16[4096,192]{0,1:T(8,128)(2,1)S(1)}, bf16[4096,192]{0,1:T(8,128)(2,1)}, u32[]{:S(2)}) %copy-start.1) | copy-done | bytes 1572888
  3.9 0.0 copy-start.2
  3.9 0.9 %copy-done.2 = s32[256,192]{0,1:T(8,128)S(1)} copy-done((s32[256,192]{0,1:T(8,128)S(1)}, s32[256,192]{0,1:T(8,128)}, u32[]{:S(2)}) %copy-start.2) | copy-done | bytes 196632
  4.9 0.0 copy-start.3
  4.9 0.9 %copy-done.3 = f32[64,384]{1,0:T(8,128)S(1)} copy-done((f32[64,384]{1,0:T(8,128)S(1)}, f32[64,384]{1,0:T(8,128)}, u32[]{:S(2)}) %copy-start.3) | copy-done | bytes 98328
  5.8 0.0 copy-start.4
  5.8 0.7 %copy-done.4 = s32[16,2]{0,1:T(2,128)S(1)} copy-done((s32[16,2]{0,1:T(2,128)S(1)}, s32[16,2]{0,1:T(2,128)}, u32[]{:S(2)}) %copy-start.4) | copy-done | bytes 152
  6.4 46.3 %shard_map.68 = (bf16[192,2048]{1,0:T(8,128)(2,1)S(1)}, f32[64,384]{1,0:T(8,128)S(1)}) custom-call(s32[2,16]{1,0:T(2,128)S(1)} %bitcast.7, bf16[4096,384]{1,0:T(8,128)(2,1)S(1)} %copy-done, bf16[192,4096]{1,0:T(8,128)(2,1)S(1)} %bitcast.4, s32[192,256]{1,0:T(8,128)S(1)} %bitcast.6, f32[64,384]{1,0:T(8,128)S(1)} %copy-done.3), custom_call_target="tpu_custom_call" | custom-call | tf_op jit(solution)/shard_map/pallas_call | solution.py:288
  52.8 0.9 %copy.9 = bf16[2048,192]{0,1:T(8,128)(2,1)} copy(bf16[2048,192]{0,1:T(8,128)(2,1)S(1)} %bitcast.5) | data formatting | bytes 1572864
  53.6 0.6 %copy.10 = f32[64,384]{1,0:T(8,128)} copy(f32[64,384]{1,0:T(8,128)S(1)} %get-tuple-element.9) | data formatting | bytes 196608
Async XLA Ops:
  0.6 1.9 %copy-start = (bf16[4096,384]{1,0:T(8,128)(2,1)S(1)}, bf16[4096,384]{1,0:T(8,128)(2,1)}, u32[]{:S(2)}) copy-start(bf16[4096,384]{1,0:T(8,128)(2,1)} %frames_ref.1) | copy-start | bytes 9437188
  2.5 1.4 %copy-start.1 = (bf16[4096,192]{0,1:T(8,128)(2,1)S(1)}, bf16[4096,192]{0,1:T(8,128)(2,1)}, u32[]{:S(2)}) copy-start(bf16[4096,192]{0,1:T(8,128)(2,1)} %param.6) | copy-start | bytes 4718596
  3.9 0.9 %copy-start.2 = (s32[256,192]{0,1:T(8,128)S(1)}, s32[256,192]{0,1:T(8,128)}, u32[]{:S(2)}) copy-start(s32[256,192]{0,1:T(8,128)} %param.7) | copy-start | bytes 589828
  4.9 0.9 %copy-start.3 = (f32[64,384]{1,0:T(8,128)S(1)}, f32[64,384]{1,0:T(8,128)}, u32[]{:S(2)}) copy-start(f32[64,384]{1,0:T(8,128)} %traces_ref.1) | copy-start | bytes 294916
  5.8 0.7 %copy-start.4 = (s32[16,2]{0,1:T(2,128)S(1)}, s32[16,2]{0,1:T(2,128)}, u32[]{:S(2)}) copy-start(s32[16,2]{0,1:T(2,128)} %param.9) | copy-start | bytes 388

commit v2 on v1

v2 whole, which is shorter than its diff:
```python
import functools

import jax
import jax.numpy as jnp
from jax import lax
from jax.experimental import pallas as pl
from jax.experimental.pallas import tpu as pltpu
from jax.sharding import PartitionSpec as P

BLOCK = 32
TILE = 16
MESH = pl.DeviceIdType.MESH
OFFSETS = (-2, -1, 1, 2)
WHOLE = 4
f32, bf16 = jnp.float32, jnp.bfloat16


def dot(a, b, dims=((1,), (0,))):
    return lax.dot_general(a, b, (dims, ((), ())), preferred_element_type=f32)


def halves(x):
    high = x.astype(bf16)
    return high, (x - high.astype(f32)).astype(bf16)


def kernel(
    owners, shares, order_hbm, frames_hbm, foot_hbm, support_hbm, traces_hbm, refined_ref, updated_ref,
    order_ref, frames_ref, support_ref, act, keep, near_traces, drive, corr, side_drive, side_corr, change,
    blk_out, blk_in, near, near_far, frames_in, part_own, part_out, part_in,
    in_sem, order_sem, a_send, a_recv, b_send, b_recv, k_send, k_recv, c_send, c_recv, d_send, d_recv,
    x_send, x_recv, y_send, y_recv, e_send, e_recv, f_send, f_recv,
):
    slab, mine = lax.axis_index("pix"), lax.axis_index("frm")
    pixels, frames_here = frames_ref.shape
    three = act.shape[0]
    width = three // 3
    sweeps = width // BLOCK
    share_rows = pixels // shares
    whole_pieces, rows_each = frames_in.shape[1], frames_in.shape[2]
    part_pieces = share_rows // rows_each - whole_pieces
    barrier = pltpu.get_barrier_semaphore()

    def present(offset):
        return slab + offset >= 0 if offset < 0 else slab + offset < owners

    def slot(offset):
        return OFFSETS.index(offset)

    def partner(d):
        return lax.rem(mine + d, shares)

    for offset in OFFSETS:
        @pl.when(present(offset))
        def _():
            pl.semaphore_signal(barrier, inc=1, device_id=(slab + offset, mine), device_id_type=MESH)
    for d in range(1, shares):
        pl.semaphore_signal(barrier, inc=1, device_id=(slab, partner(d)), device_id_type=MESH)

    groups = in_sem.shape[0] - 1
    chunk = pixels // groups

    def bring(c):
        rows = pl.ds(c * chunk, chunk)
        return [pltpu.make_async_copy(foot_hbm.at[:, rows], act.at[:, rows], in_sem.at[c, 0]),
                pltpu.make_async_copy(frames_hbm.at[rows], frames_ref.at[rows], in_sem.at[c, 1])]

    fetch_support = pltpu.make_async_copy(support_hbm, support_ref, in_sem.at[groups, 0])
    fetch_traces = pltpu.make_async_copy(traces_hbm, near_traces.at[pl.ds(width, width)], in_sem.at[groups, 1])
    fetch_order = pltpu.make_async_copy(order_hbm, order_ref, order_sem)
    fetch_support.start()
    for c in range(groups):
        for copy in bring(c):
            copy.start()
        if c == 0:
            fetch_traces.start()
            fetch_order.start()

    for offset in OFFSETS:
        @pl.when(jnp.logical_not(present(offset)))
        def _():
            for step in range(sweeps - 1):
                blk_in[step, slot(offset)] = jnp.zeros((BLOCK, frames_here), f32)
            if abs(offset) == 1:
                at = 0 if offset < 0 else 1
                side_drive[at] = jnp.zeros(side_drive.shape[1:], f32)
                side_corr[at] = jnp.zeros(side_corr.shape[1:], f32)
                row = (1 + offset) * width
                near_traces[row : row + width, :] = jnp.zeros((width, frames_here), f32)
                near[row : row + width, :] = jnp.zeros((width, frames_here), bf16)
                for d in range(1, shares):
                    near_far[d - 1, row : row + width, :] = jnp.zeros((width, frames_here), bf16)

    peers = jnp.minimum(slab, 2) + jnp.minimum(owners - 1 - slab, 2) + shares - 1
    pl.semaphore_wait(barrier, peers)

    def remote(src, dst, send, recv, to):
        return pltpu.make_async_remote_copy(
            src_ref=src, dst_ref=dst, send_sem=send, recv_sem=recv, device_id=to, device_id_type=MESH)

    def side_of(offset):
        return 1 if offset < 0 else 0

    def rows_for(offset):
        return pl.ds(0 if offset < 0 else 2 * width, width)

    def rows_there(offset):
        return pl.ds((1 - offset) * width, width)

    def send_traces(offset):
        at = side_of(offset)
        return remote(traces_hbm, near_traces.at[rows_there(offset)], a_send.at[at], a_recv.at[at], (slab + offset, mine))

    def send_drive(offset):
        at = side_of(offset)
        return remote(drive.at[rows_for(offset)], side_drive.at[at], b_send.at[at], b_recv.at[at], (slab + offset, mine))

    def send_corr(offset):
        at = side_of(offset)
        return remote(corr.at[rows_for(offset)], side_corr.at[at], k_send.at[at], k_recv.at[at], (slab + offset, mine))

    def send_block(step, offset):
        k = slot(-offset)
        return remote(blk_out.at[step], blk_in.at[step, k], c_send.at[step, k], c_recv.at[step, k], (slab + offset, mine))

    own_rows = pl.ds(width, width)

    def send_near(offset):
        at = side_of(offset)
        return remote(near.at[own_rows], near.at[rows_there(offset)], d_send.at[at], d_recv.at[at], (slab + offset, mine))

    def send_far(d):
        return remote(near.at[own_rows], near_far.at[d - 1, own_rows], x_send.at[d - 1], x_recv.at[d - 1], (slab, partner(d)))

    def relay(d, offset):
        at = side_of(offset)
        return remote(near_far.at[d - 1, own_rows], near_far.at[d - 1, rows_there(offset)],
                      y_send.at[d - 1, at], y_recv.at[d - 1, at], (slab + offset, mine))

    def first_of(who, piece):
        return pl.multiple_of(who * share_rows + piece * rows_each, rows_each)

    def send_frames(d, piece):
        return remote(frames_hbm.at[pl.ds(first_of(partner(d), piece), rows_each)], frames_in.at[d - 1, piece],
                      e_send.at[d - 1, piece], e_recv.at[d - 1, piece], (slab, partner(d)))

    def send_part(d, piece):
        return remote(part_out.at[d - 1, piece], part_in.at[d - 1, piece],
                      f_send.at[d - 1, piece], f_recv.at[d - 1, piece], (slab, partner(d)))

    def start(copy, offset):
        @pl.when(present(offset))
        def _():
            copy(offset).start()

    def arrive(copy, offset):
        @pl.when(present(-offset))
        def _():
            copy(offset).wait_recv()

    def left(copy, offset):
        @pl.when(present(offset))
        def _():
            copy(offset).wait_send()

    for offset in (-1, 1):
        start(send_traces, offset)
    for piece in range(whole_pieces):
        for d in range(1, shares):
            send_frames(d, piece).start()

    line = lax.broadcasted_iota(jnp.int32, (three, 1), 0)
    window_of = line // width
    usable = jnp.where(
        window_of == 0, (slab > 0).astype(f32), jnp.where(window_of == 2, (slab < owners - 1).astype(f32), 1.0))
    fetch_support.wait()
    supported = (support_ref[...].astype(f32) * usable).astype(bf16)
    tiles = support_ref.shape[1]
    tile_of = lax.broadcasted_iota(jnp.int32, (tiles, chunk), 1) // TILE
    tile_is = lax.broadcasted_iota(jnp.int32, (tiles, chunk), 0)
    for c in range(groups):
        rows = slice(c * chunk, (c + 1) * chunk)
        spread = (tile_is == tile_of + c * (chunk // TILE)).astype(f32).astype(bf16)
        mask = dot(supported, spread).astype(bf16)
        keep[:, rows] = mask
        from_foot, from_frames = bring(c)
        from_foot.wait()
        active = act[:, rows] * mask
        act[:, rows] = active
        together = dot(active, active, ((1,), (1,)))
        corr[...] = together if c == 0 else corr[...] + together
        from_frames.wait()
        loads = dot(active, frames_ref[rows, :])
        drive[...] = loads if c == 0 else drive[...] + loads

    for offset in (-1, 1):
        start(send_corr, offset)
    corr_high, corr_low = halves(corr[...])
    fetch_traces.wait()
    for offset in (-1, 1):
        arrive(send_traces, offset)
    high, low = halves(near_traces[...])
    both = dot(jnp.concatenate([corr_high, corr_low], axis=0), high)
    drive[...] -= both[:three] + both[three:] + dot(corr_high, low)
    for offset in (-1, 1):
        start(send_drive, offset)
    fetch_order.wait()
    for offset in (-1, 1):
        arrive(send_corr, offset)
    parts = [side_corr[0], corr[width : 2 * width, :], side_corr[1]]
    row = lax.broadcasted_iota(jnp.int32, (width, three), 0)
    column = lax.broadcasted_iota(jnp.int32, (width, three), 1)
    diagonal = jnp.zeros((width, 1), f32)
    stacked, tops = [], []
    for i, part in enumerate(parts):
        diagonal += jnp.sum(jnp.where(column == row + (2 - i) * width, part, 0.0), axis=1, keepdims=True)
        high, low = halves(part)
        tops.append(high)
        stacked.append(jnp.concatenate([high, low], axis=0))
    block_of = lax.broadcasted_iota(jnp.int32, (width, 1), 0) // BLOCK
    for offset in (-1, 1):
        arrive(send_drive, offset)
    current = near_traces[width : 2 * width, :]
    wanted = drive[width : 2 * width, :] + side_drive[0] + side_drive[1]
    rate = 1.0 / (diagonal + 1.0)

    for step in range(sweeps):
        picked = order_ref[step, slab]
        after = jnp.where(block_of == picked, jnp.maximum(current + wanted * rate, 0.0), current)
        if step < sweeps - 1:
            moved = after - current
            block = jnp.zeros((BLOCK, frames_here), f32)
            for k in range(sweeps):
                block = jnp.where(picked == k, moved[k * BLOCK : (k + 1) * BLOCK], block)
            blk_out[step] = block
            for offset in OFFSETS:
                start(functools.partial(send_block, step), offset)
            change[2 * width : 3 * width, :] = moved
            for offset in OFFSETS:
                arrive(functools.partial(send_block, step), offset)
            for offset in OFFSETS:
                there = jnp.clip(slab + offset, 0, owners - 1)
                first = (2 + offset) * width
                news = jnp.concatenate([blk_in[step, slot(offset)]] * sweeps, axis=0)
                change[first : first + width, :] = jnp.where(block_of == order_ref[step, there], news, 0.0)
            high, low = halves(change[...])
            for i in range(3):
                span = slice(i * width, i * width + three)
                both = dot(stacked[i], high[span])
                wanted -= both[:width] + both[width:] + dot(tops[i], low[span])
        current = after
    near[width : 2 * width, :] = current.astype(bf16)
    for offset in (-1, 1):
        start(send_near, offset)
    for d in range(1, shares):
        send_far(d).start()
    updated_ref[...] = current

    for offset in (-1, 1):
        arrive(send_near, offset)
    traces_near = near[...]
    over_frames = ((1,), (1,))
    gram_here = dot(traces_near, traces_near, over_frames)
    both_here = jnp.concatenate(halves(gram_here), axis=0)

    def residual(first):
        rows = pl.ds(first, rows_each)
        fitted = dot(both_here, act[:, rows])
        return dot(traces_near, frames_ref[rows, :], over_frames) - fitted[:three] - fitted[three:]

    for piece in range(part_pieces):
        for d in range(1, shares):
            part_out[d - 1, piece] = residual(first_of(partner(d), whole_pieces + piece)).astype(bf16)
            send_part(d, piece).start()
        if piece == 0:
            for d in range(1, shares):
                send_far(d).wait_recv()
                for offset in (-1, 1):
                    start(functools.partial(relay, d), offset)
    for piece in range(part_pieces):
        part_own[piece] = residual(first_of(mine, whole_pieces + piece))

    gram = gram_here
    for d in range(1, shares):
        for offset in (-1, 1):
            arrive(functools.partial(relay, d), offset)
        gram += dot(near_far[d - 1], near_far[d - 1], over_frames)
    grow = lax.broadcasted_iota(jnp.int32, (three, three), 0)
    gcol = lax.broadcasted_iota(jnp.int32, (three, three), 1)
    rate = 1.0 / (jnp.sum(jnp.where(grow == gcol, gram, 0.0), axis=1, keepdims=True) + 1.0)
    gram_high, gram_low = halves(gram)
    gram_both = jnp.concatenate([gram_high, gram_low], axis=0)
    line_block = lax.rem(line, width) // BLOCK
    picks = []
    for step in range(sweeps):
        chosen = [order_ref[step, jnp.clip(slab - 1 + w, 0, owners - 1)] for w in range(3)]
        chosen = jnp.where(window_of == 0, chosen[0], jnp.where(window_of == 1, chosen[1], chosen[2]))
        picks.append(line_block == chosen)

    def refine(piece, left_over):
        here = pl.ds(first_of(mine, piece), rows_each)
        shaped = act[:, here].astype(f32)
        mask = keep[:, here].astype(f32)
        for step in range(sweeps):
            after = jnp.where(picks[step], jnp.maximum(shaped + left_over * rate, 0.0) * mask, shaped)
            if step < sweeps - 1:
                moved, rest = halves(after - shaped)
                lost = dot(gram_both, moved)
                left_over = left_over - (lost[:three] + lost[three:] + dot(gram_high, rest))
            shaped = after
        refined_ref[:, piece * rows_each : (piece + 1) * rows_each] = shaped.astype(bf16)

    for piece in range(whole_pieces):
        here = pl.ds(first_of(mine, piece), rows_each)
        fitted = dot(gram_both, act[:, here])
        left_over = dot(traces_near, frames_ref[here, :], over_frames) - fitted[:three] - fitted[three:]
        for d in range(1, shares):
            send_frames(d, piece).wait_recv()
            left_over += dot(near_far[d - 1], frames_in[d - 1, piece], over_frames)
        refine(piece, left_over)
    for piece in range(part_pieces):
        left_over = part_own[piece]
        for d in range(1, shares):
            send_part(d, piece).wait_recv()
            left_over += part_in[d - 1, piece].astype(f32)
        refine(whole_pieces + piece, left_over)

    for offset in OFFSETS:
        for step in range(sweeps - 1):
            left(functools.partial(send_block, step), offset)
    for offset in (-1, 1):
        for copy in (send_traces, send_drive, send_corr, send_near):
            left(copy, offset)
        for d in range(1, shares):
            left(functools.partial(relay, d), offset)
    for d in range(1, shares):
        send_far(d).wait_send()
        for piece in range(whole_pieces):
            send_frames(d, piece).wait_send()
        for piece in range(part_pieces):
            send_part(d, piece).wait_send()


def shards(owners, shares, frames, footprints, support, traces, block_order):
    pixels, frames_here = frames.shape
    width = traces.shape[0]
    three = 3 * width
    rounds = max(width // BLOCK - 1, 1)
    share_rows = pixels // shares
    rows_each = min(share_rows // 2, 256)
    pieces = share_rows // rows_each
    whole_pieces = pieces * WHOLE // 8
    part_pieces = pieces - whole_pieces
    others = max(shares - 1, 1)
    groups = 4
    vmem, dma = pltpu.VMEM, pltpu.SemaphoreType.DMA
    refined, updated = pl.pallas_call(
        functools.partial(kernel, owners, shares),
        out_shape=(
            jax.ShapeDtypeStruct((three, share_rows), bf16),
            jax.ShapeDtypeStruct(traces.shape, f32),
        ),
        in_specs=[pl.BlockSpec(memory_space=pl.ANY)] * 5,
        out_specs=(pl.BlockSpec(memory_space=vmem), pl.BlockSpec(memory_space=vmem)),
        scratch_shapes=[
            pltpu.SMEM(block_order.shape[::-1], jnp.int32),
            vmem(frames.shape, bf16),
            vmem(support.shape[::-1], jnp.int32),
            vmem((three, pixels), bf16),
            vmem((three, pixels), bf16),
            vmem((three, frames_here), f32),
            vmem((three, frames_here), f32),
            vmem((three, three), f32),
            vmem((2, width, frames_here), f32),
            vmem((2, width, three), f32),
            vmem((5 * width, frames_here), f32),
            vmem((rounds, BLOCK, frames_here), f32),
            vmem((rounds, 4, BLOCK, frames_here), f32),
            vmem((three, frames_here), bf16),
            vmem((others, three, frames_here), bf16),
            vmem((others, whole_pieces, rows_each, frames_here), bf16),
            vmem((part_pieces, three, rows_each), f32),
            vmem((others, part_pieces, three, rows_each), bf16),
            vmem((others, part_pieces, three, rows_each), bf16),
            dma((groups + 1, 2)), dma,
            dma((2,)), dma((2,)), dma((2,)), dma((2,)), dma((2,)), dma((2,)),
            dma((rounds, 4)), dma((rounds, 4)), dma((2,)), dma((2,)),
            dma((others,)), dma((others,)), dma((others, 2)), dma((others, 2)),
            dma((others, whole_pieces)), dma((others, whole_pieces)),
            dma((others, part_pieces)), dma((others, part_pieces)),
        ],
        compiler_params=pltpu.CompilerParams(
            collective_id=0, has_side_effects=True, vmem_limit_bytes=56 * 1024 * 1024
        ),
    )(block_order.T, frames, footprints.T, support.T, traces)
    return refined.T, updated


def solution(mesh):
    in_specs = (P("pix", "frm"), P("pix", None), P("pix", None), P("pix", "frm"), P())
    out_specs = (P(("pix", "frm"), None), P("pix", "frm"))
    body = functools.partial(shards, mesh.shape["pix"], mesh.shape["frm"])
    return jax.shard_map(body, mesh=mesh, in_specs=in_specs, out_specs=out_specs, check_vma=False)
```

time: 54.5 us -> 38.3 us (0.70)
  the two profiles are of different devices: /device:TPU:16 before, /device:TPU:0 now
where the time goes in v2:
time: 38.3 us; the launch traced here: 38.1 us
  Pallas kernels  33.9 us (89%)
  local copies, waits for them, and re-layouts  3.63 us (9%)
  between operations  0.64 us (2%)
    pallas_call x1, Pallas kernels, shards(): pl.pallas_call(functools.partial(kernel, owners, shares), out_shape=(jax....  33.9 us
    unnamed x2, local copies, waits for them, and re-layouts  3.63 us

profile of v2, /device:TPU:0, one launch (start us, length us, event | category | flops | bytes accessed | tf_op | source)
XLA Modules:
  0.0 38.1 jit_solution(2460224543098894915)
XLA Ops:
  0.6 33.9 %shard_map.68 = (bf16[192,2048]{1,0:T(8,128)(2,1)}, f32[64,384]{1,0:T(8,128)}) custom-call(s32[2,16]{1,0:T(2,128)} %bitcast.7, bf16[4096,384]{1,0:T(8,128)(2,1)} %frames_hbm.1, bf16[192,4096]{1,0:T(8,128)(2,1)} %bitcast.4, s32[192,256]{1,0:T(8,128)} %bitcast.6, f32[64,384]{1,0:T(8,128)} %traces_hbm.1), custom_call_target="tpu_custom_call" | custom-call | tf_op jit(solution)/shard_map/pallas_call | solution.py:357
  34.5 2.1 %copy.9 = bf16[2048,192]{0,1:T(8,128)(2,1)} copy(bf16[2048,192]{0,1:T(8,128)(2,1)} %bitcast.5) | data formatting | bytes 1572864
  36.6 1.5 %copy.10 = f32[64,384]{1,0:T(8,128)} copy(f32[64,384]{1,0:T(8,128)} %get-tuple-element.9) | data formatting | bytes 196608

commit v3 on v2

--- a/solution.py
+++ b/solution.py
@@ -25,10 +25,10 @@
 
 
 def kernel(
-    owners, shares, order_hbm, frames_hbm, foot_hbm, support_hbm, traces_hbm, refined_ref, updated_ref,
+    owners, shares, order_hbm, frames_hbm, foot_hbm, support_hbm, traces_hbm, refined_hbm, updated_hbm,
     order_ref, frames_ref, support_ref, act, keep, near_traces, drive, corr, side_drive, side_corr, change,
     blk_out, blk_in, near, near_far, frames_in, part_own, part_out, part_in,
-    in_sem, order_sem, a_send, a_recv, b_send, b_recv, k_send, k_recv, c_send, c_recv, d_send, d_recv,
+    refined_ref, updated_ref, out_sem, in_sem, order_sem, a_send, a_recv, b_send, b_recv, k_send, k_recv, c_send, c_recv, d_send, d_recv,
     x_send, x_recv, y_send, y_recv, e_send, e_recv, f_send, f_recv,
 ):
     slab, mine = lax.axis_index("pix"), lax.axis_index("frm")
@@ -255,6 +255,7 @@
     for d in range(1, shares):
         send_far(d).start()
     updated_ref[...] = current
+    pltpu.make_async_copy(updated_ref, updated_hbm, out_sem.at[whole_pieces + part_pieces]).start()
 
     for offset in (-1, 1):
         arrive(send_near, offset)
@@ -297,6 +298,10 @@
         chosen = jnp.where(window_of == 0, chosen[0], jnp.where(window_of == 1, chosen[1], chosen[2]))
         picks.append(line_block == chosen)
 
+    def deposit(piece):
+        span = pl.ds(piece * rows_each, rows_each)
+        return pltpu.make_async_copy(refined_ref.at[:, span], refined_hbm.at[:, span], out_sem.at[piece])
+
     def refine(piece, left_over):
         here = pl.ds(first_of(mine, piece), rows_each)
         shaped = act[:, here].astype(f32)
@@ -309,6 +314,7 @@
                 left_over = left_over - (lost[:three] + lost[three:] + dot(gram_high, rest))
             shaped = after
         refined_ref[:, piece * rows_each : (piece + 1) * rows_each] = shaped.astype(bf16)
+        deposit(piece).start()
 
     for piece in range(whole_pieces):
         here = pl.ds(first_of(mine, piece), rows_each)
@@ -325,6 +331,9 @@
             left_over += part_in[d - 1, piece].astype(f32)
         refine(whole_pieces + piece, left_over)
 
+    for piece in range(whole_pieces + part_pieces):
+        deposit(piece).wait()
+    pltpu.make_async_copy(updated_ref, updated_hbm, out_sem.at[whole_pieces + part_pieces]).wait()
     for offset in OFFSETS:
         for step in range(sweeps - 1):
             left(functools.partial(send_block, step), offset)
@@ -339,6 +348,34 @@
             send_frames(d, piece).wait_send()
         for piece in range(part_pieces):
             send_part(d, piece).wait_send()
+
+
+def deliver_kernel(refined_ref, updated_ref, refined_out, updated_out, refined_held, updated_held, sem):
+    rows = refined_ref.shape[0] // 4
+    moves = [(updated_ref, updated_held, updated_out)]
+    for i in range(4):
+        part = pl.ds(i * rows, rows)
+        moves.append((refined_ref.at[part], refined_held.at[part], refined_out.at[part]))
+    inward = [pltpu.make_async_copy(a, b, sem.at[0, i]) for i, (a, b, c) in enumerate(moves)]
+    outward = [pltpu.make_async_copy(b, c, sem.at[1, i]) for i, (a, b, c) in enumerate(moves)]
+    for copy in inward:
+        copy.start()
+    for copy, onward in zip(inward, outward):
+        copy.wait()
+        onward.start()
+    for copy in outward:
+        copy.wait()
+
+
+def deliver(refined, updated):
+    like = [jax.ShapeDtypeStruct(x.shape, x.dtype) for x in (refined, updated)]
+    anywhere = pl.BlockSpec(memory_space=pl.ANY)
+    refined, updated = pl.pallas_call(
+        deliver_kernel, out_shape=like, in_specs=[anywhere] * 2, out_specs=[anywhere] * 2,
+        scratch_shapes=[pltpu.VMEM(x.shape, x.dtype) for x in like] + [pltpu.SemaphoreType.DMA((2, 5))],
+        compiler_params=pltpu.CompilerParams(vmem_limit_bytes=56 * 1024 * 1024),
+    )(refined, updated)
+    return refined.T, updated
 
 
 def shards(owners, shares, frames, footprints, support, traces, block_order):
@@ -361,7 +398,7 @@
             jax.ShapeDtypeStruct(traces.shape, f32),
         ),
         in_specs=[pl.BlockSpec(memory_space=pl.ANY)] * 5,
-        out_specs=(pl.BlockSpec(memory_space=vmem), pl.BlockSpec(memory_space=vmem)),
+        out_specs=(pl.BlockSpec(memory_space=pl.ANY), pl.BlockSpec(memory_space=pl.ANY)),
         scratch_shapes=[
             pltpu.SMEM(block_order.shape[::-1], jnp.int32),
             vmem(frames.shape, bf16),
@@ -382,6 +419,7 @@
             vmem((part_pieces, three, rows_each), f32),
             vmem((others, part_pieces, three, rows_each), bf16),
             vmem((others, part_pieces, three, rows_each), bf16),
+            vmem((three, share_rows), bf16), vmem(traces.shape, f32), dma((pieces + 1,)),
             dma((groups + 1, 2)), dma,
             dma((2,)), dma((2,)), dma((2,)), dma((2,)), dma((2,)), dma((2,)),
             dma((rounds, 4)), dma((rounds, 4)), dma((2,)), dma((2,)),
@@ -393,7 +431,7 @@
             collective_id=0, has_side_effects=True, vmem_limit_bytes=56 * 1024 * 1024
         ),
     )(block_order.T, frames, footprints.T, support.T, traces)
-    return refined.T, updated
+    return deliver(refined, updated)
 
 
 def solution(mesh):

time: 38.3 us -> 36.5 us (0.953)
  local copies, waits for them, and re-layouts: 3.63 us -> 0 us
  Pallas kernels: 33.9 us -> 35.7 us
    unnamed x2 -> x0, local copies, waits for them, and re-layouts: 3.63 us -> none
    pallas_call x0 -> x1, Pallas kernels: none -> 2.03 us  [deliver(): pl.pallas_call(deliver_kernel, out_shape=like, in_specs=[anywhere] * 2, o...]
where the time goes in v3:
time: 36.5 us; the launch traced here: 36.3 us
  Pallas kernels  35.7 us (98%)
  between operations  0.64 us (2%)
    pallas_call x1, Pallas kernels, shards(): pl.pallas_call(functools.partial(kernel, owners, shares), out_shape=(jax....  33.7 us
    pallas_call x1, Pallas kernels, deliver(): pl.pallas_call(deliver_kernel, out_shape=like, in_specs=[anywhere] * 2, o...  2.03 us

profile of v3, /device:TPU:0, one launch (start us, length us, event | category | flops | bytes accessed | tf_op | source)
XLA Modules:
  0.0 36.3 jit_solution(12433934881922487405)
XLA Ops:
  0.6 33.7 %shard_map.68 = (bf16[192,2048]{1,0:T(8,128)(2,1)}, f32[64,384]{1,0:T(8,128)}) custom-call(s32[2,16]{1,0:T(2,128)} %bitcast.6, bf16[4096,384]{1,0:T(8,128)(2,1)} %frames_hbm.1, bf16[192,4096]{1,0:T(8,128)(2,1)} %bitcast.4, s32[192,256]{1,0:T(8,128)} %bitcast.5, f32[64,384]{1,0:T(8,128)} %traces_hbm.1), custom_call_target="tpu_custom_call" | custom-call | tf_op jit(solution)/shard_map/pallas_call | solution.py:394
  34.3 2.0 %shard_map.69 = (bf16[192,2048]{1,0:T(8,128)(2,1)}, f32[64,384]{1,0:T(8,128)}) custom-call(bf16[192,2048]{1,0:T(8,128)(2,1)} %get-tuple-element.6.refined_ref, f32[64,384]{1,0:T(8,128)} %get-tuple-element.7.updated_ref), custom_call_target="tpu_custom_call" | custom-call | tf_op jit(solution)/shard_map/pallas_call | solution.py:373

commit v4 on v3

--- a/solution.py
+++ b/solution.py
@@ -11,7 +11,7 @@
 TILE = 16
 MESH = pl.DeviceIdType.MESH
 OFFSETS = (-2, -1, 1, 2)
-WHOLE = 4
+WHOLE = 7
 f32, bf16 = jnp.float32, jnp.bfloat16
 
 
@@ -384,9 +384,9 @@
     three = 3 * width
     rounds = max(width // BLOCK - 1, 1)
     share_rows = pixels // shares
-    rows_each = min(share_rows // 2, 256)
+    rows_each = min(share_rows // 2, 128)
     pieces = share_rows // rows_each
-    whole_pieces = pieces * WHOLE // 8
+    whole_pieces = max(pieces * WHOLE // 16, 1)
     part_pieces = pieces - whole_pieces
     others = max(shares - 1, 1)
     groups = 4

time: 36.5 us -> 36.1 us (0.989)
  Pallas kernels: 35.7 us -> 35.2 us
    pallas_call x1, Pallas kernels: 33.7 us -> 33.2 us  [shards(): pl.pallas_call(functools.partial(kernel, owners, shares), out_shape=(jax....]
where the time goes in v4:
time: 36.1 us; the launch traced here: 35.8 us
  Pallas kernels  35.2 us (98%)
  between operations  0.64 us (2%)
    pallas_call x1, Pallas kernels, shards(): pl.pallas_call(functools.partial(kernel, owners, shares), out_shape=(jax....  33.2 us
    pallas_call x1, Pallas kernels, deliver(): pl.pallas_call(deliver_kernel, out_shape=like, in_specs=[anywhere] * 2, o...  2.03 us

profile of v4, /device:TPU:0, one launch (start us, length us, event | category | flops | bytes accessed | tf_op | source)
XLA Modules:
  0.0 35.8 jit_solution(9352360519558934798)
XLA Ops:
  0.6 33.2 %shard_map.68 = (bf16[192,2048]{1,0:T(8,128)(2,1)}, f32[64,384]{1,0:T(8,128)}) custom-call(s32[2,16]{1,0:T(2,128)} %bitcast.6, bf16[4096,384]{1,0:T(8,128)(2,1)} %frames_hbm.1, bf16[192,4096]{1,0:T(8,128)(2,1)} %bitcast.4, s32[192,256]{1,0:T(8,128)} %bitcast.5, f32[64,384]{1,0:T(8,128)} %traces_hbm.1), custom_call_target="tpu_custom_call" | custom-call | tf_op jit(solution)/shard_map/pallas_call | solution.py:394
  33.8 2.0 %shard_map.69 = (bf16[192,2048]{1,0:T(8,128)(2,1)}, f32[64,384]{1,0:T(8,128)}) custom-call(bf16[192,2048]{1,0:T(8,128)(2,1)} %get-tuple-element.6.refined_ref, f32[64,384]{1,0:T(8,128)} %get-tuple-element.7.updated_ref), custom_call_target="tpu_custom_call" | custom-call | tf_op jit(solution)/shard_map/pallas_call | solution.py:373
